TPU v7x, 32 devices: a whole 2x2x4 slice. The times are simulated.
32 devices in a mesh: rows: 16 (over z, y, x), keys: 2 (over core).
Axes of the slice: x: 2, y: 2, z: 4, core: 2. Of those that a mesh axis runs over, the one named last changes fastest.
Arguments:
- tokens: bfloat16 [16, 1024, 768], P('rows', 'keys'), may hold values from -6 to 6
- seg_ids: int32 [16, 1024], P('rows'), may hold values from 0 to 7, as said below
- doc_starts: int32 [16, 1024], P('rows', 'keys'), may hold values from 0 to 1, as said below
- gain_in: float32 [768], replicated, may hold values from 0.1 to 1.9
- shift_in: float32 [768], replicated, may hold values from -3 to 3
- w_query: bfloat16 [768, 768], replicated, may hold values from -0.21875 to 0.21875
- w_key: bfloat16 [768, 768], replicated, may hold values from -0.21875 to 0.21875
- w_value: bfloat16 [768, 768], replicated, may hold values from -0.21875 to 0.21875
- w_out: bfloat16 [768, 768], replicated, may hold values from -0.625 to 0.625
- gain_mid: float32 [768], replicated, may hold values from 0.1 to 1.9
- shift_mid: float32 [768], replicated, may hold values from -3 to 3
- w_up: bfloat16 [768, 3072], replicated, may hold values from -0.21875 to 0.21875
- w_down: bfloat16 [3072, 768], replicated, may hold values from -0.109375 to 0.109375
- out_grad: bfloat16 [16, 1024, 768], P('rows', 'keys'), may hold values from -6 to 6
Outputs:
- output: bfloat16 [16, 1024, 768], P('rows', 'keys')
- input_grad: bfloat16 [16, 1024, 768], P('rows', 'keys')
- key_share: float32 [16, 1024], P('rows', 'keys')
- grad_gain_in: float32 [768], P('rows')
- grad_shift_in: float32 [768], P('rows')
- grad_w_query: float32 [768, 768], P('rows')
- grad_w_key: float32 [768, 768], P('rows')
- grad_w_value: float32 [768, 768], P('rows')
- grad_w_out: float32 [768, 768], P('rows')
- grad_gain_mid: float32 [768], P('rows')
- grad_shift_mid: float32 [768], P('rows')
- grad_w_up: float32 [768, 3072], P('rows')
- grad_w_down: float32 [3072, 768], P('rows')
Inputs may be any that keep to these rules, and one draw needn't show every extreme that they name: `seg_ids`: within each row the ids begin at 0 and rise by one at each document's first token; they never fall. Every row holds exactly 8 documents. `doc_starts`: 1 exactly at a row's first token and where seg_ids differs from the previous token's, else 0.
All inputs are finite; a program needn't handle non-finite values.
Results may differ from a plain program's by a relative error of at most 0.019.
Values may be sent and summed in bfloat16 or wider, within the bound.
A program may use at most 192 MiB of HBM per device.

v0:
```python
import jax
import jax.numpy as jnp
from jax import lax
from jax.sharding import PartitionSpec as P

HEAD = 64


EPS = 1e-05
NEGATIVE = -1e30
HIGHEST = lax.Precision.HIGHEST
SELECT_SHIFT = 4.0


def joined(value, axis, join):
    pieces = jax.tree.map(lambda part: lax.all_gather(part, axis), value)
    head = jax.tree.map(lambda part: part[0], pieces)
    tail = jax.tree.map(lambda part: part[1:], pieces)
    so_far, _ = lax.scan(lambda so_far, section: (join(so_far, section), None), head, tail)
    return so_far


def layer_norm(field, gain_vec, offset):
    center = field - jnp.mean(field, -1, keepdims=True)
    inverse = lax.rsqrt(jnp.mean(center * center, -1, keepdims=True) + EPS)
    unit_rows = center * inverse
    return (unit_rows * gain_vec + offset, unit_rows, inverse)


def norm_back(gradient, unit_rows, inverse, gain_vec):
    scaled = gradient * gain_vec
    return inverse * (
        scaled
        - jnp.mean(scaled, -1, keepdims=True)
        - unit_rows * jnp.mean(scaled * unit_rows, -1, keepdims=True)
    )


def gelu_tanh(field):
    return jax.nn.gelu(field, approximate=True)


def transpose_dot(left, right):
    return jnp.einsum("ti,to->io", left, right, preferred_element_type=jnp.float32)


def right_dot(left, right):
    return jnp.einsum("ti,oi->to", left, right, preferred_element_type=jnp.float32)


def block_masks(context, seg_block, block_index):
    key_vecs, seg_keys, free_keys, key_pos, block_len, score_scale = context
    query_pos = block_index * block_len + jnp.arange(block_len)
    same_doc = seg_block[:, None] == seg_keys[None, :]
    allowed = same_doc & (key_pos[None, :] <= query_pos[:, None])
    after_key = same_doc & (key_pos[None, :] < query_pos[:, None])
    return (allowed, after_key, after_key & free_keys[None, :])


def block_scores(context, query_blk):
    key_vecs = context[0]
    return (
        jnp.einsum("qhd,khd->hqk", query_blk, key_vecs, preferred_element_type=jnp.float32)
        * context[5]
    )


def recompute(context, query_blk, seg_block, block_index, cumulated_blk):
    allowed, after_key, select = block_masks(context, seg_block, block_index)
    scores = block_scores(context, query_blk)
    logits = jnp.where(allowed[None], scores - cumulated_blk[None], NEGATIVE)
    return (scores, logits, select)


def block_inputs(query_rows, seg_row, block_len):
    blocks = query_rows.shape[0] // block_len
    return (
        query_rows.reshape(blocks, block_len, query_rows.shape[1], query_rows.shape[2]),
        seg_row.reshape(blocks, block_len),
        jnp.arange(blocks),
    )


def head_blocks(stat_rows, block_len):
    return stat_rows.reshape(stat_rows.shape[0], -1, block_len).transpose(1, 0, 2)


def forward_stats(context, query_rows, seg_row):
    block_len = context[4]
    key_len = context[0].shape[0]
    row_len = query_rows.shape[0]
    places = jnp.arange(block_len)
    lower_ones = (places[None, :] < places[:, None]).astype(jnp.float32)

    def scan_step(carried, inputs):
        running, numerator, pair_count = carried
        query_blk, seg_block, block_index = inputs
        allowed, after_key, select = block_masks(context, seg_block, block_index)
        scores = block_scores(context, query_blk)
        chosen = jnp.where(select, jax.nn.softplus(scores[0] - SELECT_SHIFT), 0.0)
        cumulated = running[None, :] + jnp.dot(lower_ones, chosen, precision=HIGHEST)
        logits = jnp.where(allowed[None], scores - cumulated[None], NEGATIVE)
        maxima = jnp.max(logits, -1)
        totals = jnp.sum(jnp.exp(logits - maxima[..., None]), -1)
        numerator = numerator + jnp.sum(
            jnp.where(after_key, jax.nn.sigmoid(cumulated - 2.0), 0.0), 0
        )
        pair_count = pair_count + jnp.sum(after_key.astype(jnp.float32), 0)
        return ((running + jnp.sum(chosen, 0), numerator, pair_count), (cumulated, maxima, totals))

    zeros = jnp.zeros((key_len,), jnp.float32)
    (_, numerator, pair_count), (cumulated, maxima, totals) = lax.scan(
        scan_step, (zeros, zeros, zeros), block_inputs(query_rows, seg_row, block_len)
    )
    head_count = maxima.shape[1]
    maxima = maxima.transpose(1, 0, 2).reshape(head_count, row_len)
    totals = totals.transpose(1, 0, 2).reshape(head_count, row_len)
    share = numerator / jnp.maximum(pair_count, 1.0)
    return (cumulated.reshape(row_len, key_len), maxima, totals, share)


def forward_values(context, values, query_rows, seg_row, cumulated, log_sums):
    block_len = context[4]
    blocks = query_rows.shape[0] // block_len

    def scan_step(carried, inputs):
        query_blk, seg_block, block_index, cumulated_blk, log_blk = inputs
        scores, logits, select = recompute(
            context, query_blk, seg_block, block_index, cumulated_blk
        )
        weights = jnp.exp(logits - log_blk[..., None]).astype(jnp.bfloat16)
        head_sums = jnp.einsum("hqk,khd->qhd", weights, values, preferred_element_type=jnp.float32)
        return (carried, head_sums.reshape(block_len, -1))

    inputs = block_inputs(query_rows, seg_row, block_len) + (
        cumulated.reshape(blocks, block_len, -1),
        head_blocks(log_sums, block_len),
    )
    _, outputs = lax.scan(scan_step, jnp.zeros((), jnp.float32), inputs)
    return outputs.reshape(query_rows.shape[0], -1)


def delta_terms(context, values, query_rows, seg_row, cumulated, log_sums, dout_rows):
    block_len = context[4]
    blocks = query_rows.shape[0] // block_len

    def scan_step(carried, inputs):
        query_blk, seg_block, block_index, cumulated_blk, log_blk, dout_blk = inputs
        scores, logits, select = recompute(
            context, query_blk, seg_block, block_index, cumulated_blk
        )
        weights = jnp.exp(logits - log_blk[..., None])
        grad_weights = jnp.einsum(
            "qhd,khd->hqk", dout_blk, values, preferred_element_type=jnp.float32
        )
        return (carried, jnp.sum(weights * grad_weights, -1))

    inputs = block_inputs(query_rows, seg_row, block_len) + (
        cumulated.reshape(blocks, block_len, -1),
        head_blocks(log_sums, block_len),
        dout_rows.reshape(blocks, block_len, dout_rows.shape[1], dout_rows.shape[2]),
    )
    _, terms = lax.scan(scan_step, jnp.zeros((), jnp.float32), inputs)
    return terms.transpose(1, 0, 2).reshape(terms.shape[1], -1)


def backward_row(context, values, query_rows, seg_row, cumulated, log_sums, dout_rows, deltas):
    key_vecs, block_len, score_scale = (context[0], context[4], context[5])
    blocks = query_rows.shape[0] // block_len
    places = jnp.arange(block_len)
    upper_ones = (places[None, :] > places[:, None]).astype(jnp.float32)

    def scan_step(carried, inputs):
        later_sum, key_grad, value_grad = carried
        query_blk, seg_block, block_index, cumulated_blk, log_blk, dout_blk, delta_blk = inputs
        scores, logits, select = recompute(
            context, query_blk, seg_block, block_index, cumulated_blk
        )
        weights = jnp.exp(logits - log_blk[..., None])
        grad_weights = jnp.einsum(
            "qhd,khd->hqk", dout_blk, values, preferred_element_type=jnp.float32
        )
        grad_logits = weights * (grad_weights - delta_blk[..., None])
        grad_cumulated = -jnp.sum(grad_logits, 0)
        grad_chosen = later_sum[None, :] + jnp.dot(upper_ones, grad_cumulated, precision=HIGHEST)
        extra = jnp.where(select, grad_chosen * jax.nn.sigmoid(scores[0] - SELECT_SHIFT), 0.0)
        grad_scores = grad_logits.at[0].add(extra).astype(jnp.bfloat16)
        query_grad = (
            jnp.einsum("hqk,khd->qhd", grad_scores, key_vecs, preferred_element_type=jnp.float32)
            * score_scale
        )
        key_grad = (
            key_grad
            + jnp.einsum("hqk,qhd->khd", grad_scores, query_blk, preferred_element_type=jnp.float32)
            * score_scale
        )
        value_grad = value_grad + jnp.einsum(
            "hqk,qhd->khd",
            weights.astype(jnp.bfloat16),
            dout_blk,
            preferred_element_type=jnp.float32,
        )
        return (
            (later_sum + jnp.sum(grad_cumulated, 0), key_grad, value_grad),
            query_grad.reshape(block_len, -1),
        )

    inputs = block_inputs(query_rows, seg_row, block_len) + (
        cumulated.reshape(blocks, block_len, -1),
        head_blocks(log_sums, block_len),
        dout_rows.reshape(blocks, block_len, dout_rows.shape[1], dout_rows.shape[2]),
        head_blocks(deltas, block_len),
    )
    zeros = jnp.zeros(key_vecs.shape, jnp.float32)
    start_sum = jnp.zeros((key_vecs.shape[0],), jnp.float32)
    (_, key_grad, value_grad), query_grad = lax.scan(
        scan_step, (start_sum, zeros, zeros), inputs, reverse=True
    )
    return (query_grad.reshape(query_rows.shape[0], -1), key_grad, value_grad)


def combine_stats(first_stats, second_stats):
    maxima = jnp.maximum(first_stats[0], second_stats[0])
    totals = first_stats[1] * jnp.exp(first_stats[0] - maxima) + second_stats[1] * jnp.exp(
        second_stats[0] - maxima
    )
    return (maxima, totals)


def body(
    tokens,
    seg_ids,
    doc_starts,
    gain_in,
    shift_in,
    w_query,
    w_key,
    w_value,
    w_out,
    gain_mid,
    shift_mid,
    w_up,
    w_down,
    out_grad,
):
    row_count, key_len, width = tokens.shape
    row_len = seg_ids.shape[1]
    head_count = width // HEAD
    score_scale = HEAD ** (-0.5)
    block_len = min(512, row_len)
    key_first = lax.axis_index("keys") * key_len
    key_pos = key_first + jnp.arange(key_len)
    seg_keys = lax.dynamic_slice_in_dim(seg_ids, key_first, key_len, 1)
    free_keys = doc_starts == 0
    token_count = row_count * key_len
    flat_in = tokens.reshape(token_count, width).astype(jnp.float32)
    normed_in, unit_in, inverse_in = layer_norm(flat_in, gain_in, shift_in)
    low_in = normed_in.astype(jnp.bfloat16)
    queries = jnp.dot(low_in, w_query, preferred_element_type=jnp.float32).astype(jnp.bfloat16)
    key_vecs = (
        jnp.dot(low_in, w_key, preferred_element_type=jnp.float32)
        .astype(jnp.bfloat16)
        .reshape(row_count, key_len, head_count, HEAD)
    )
    values = (
        jnp.dot(low_in, w_value, preferred_element_type=jnp.float32)
        .astype(jnp.bfloat16)
        .reshape(row_count, key_len, head_count, HEAD)
    )
    query_all = lax.all_gather(
        queries.reshape(row_count, key_len, width), "keys", axis=1, tiled=True
    ).reshape(row_count, row_len, head_count, HEAD)
    row_index = 0
    context = (
        key_vecs[row_index],
        seg_keys[row_index],
        free_keys[row_index],
        key_pos,
        block_len,
        score_scale,
    )
    contexts = [context]
    cumulated, maxima, totals, share = forward_stats(
        context, query_all[row_index], seg_ids[row_index]
    )
    cumulated_list = [cumulated]
    maxima_list = [maxima]
    totals_list = [totals]
    share_list = [share]
    maxima, totals = joined((jnp.stack(maxima_list), jnp.stack(totals_list)), "keys", combine_stats)
    log_sums = maxima + jnp.log(totals)
    head_parts = jnp.stack(
        [
            forward_values(
                contexts[0], values[0], query_all[0], seg_ids[0], cumulated_list[0], log_sums[0]
            )
        ]
    )
    head_out = lax.psum_scatter(
        head_parts.astype(jnp.bfloat16), "keys", scatter_dimension=1, tiled=True
    ).astype(jnp.float32)
    low_out = head_out.reshape(token_count, width).astype(jnp.bfloat16)
    resid = flat_in + jnp.dot(low_out, w_out, preferred_element_type=jnp.float32)
    normed_mid, unit_mid, inverse_mid = layer_norm(resid, gain_mid, shift_mid)
    low_mid = normed_mid.astype(jnp.bfloat16)
    upward = jnp.dot(low_mid, w_up, preferred_element_type=jnp.float32)
    hidden = gelu_tanh(upward).astype(jnp.bfloat16)
    output = (resid + jnp.dot(hidden, w_down, preferred_element_type=jnp.float32)).astype(
        jnp.bfloat16
    )
    cotangent = out_grad.reshape(token_count, width)
    grad_down = transpose_dot(hidden, cotangent)
    grad_hidden = right_dot(cotangent, w_down)
    _, pullback = jax.vjp(gelu_tanh, upward)
    grad_upward = pullback(grad_hidden)[0].astype(jnp.bfloat16)
    grad_up = transpose_dot(low_mid, grad_upward)
    grad_mid = right_dot(grad_upward, w_up)
    grad_resid = cotangent.astype(jnp.float32) + norm_back(
        grad_mid, unit_mid, inverse_mid, gain_mid
    )
    low_resid = grad_resid.astype(jnp.bfloat16)
    grad_outproj = transpose_dot(low_out, low_resid)
    grad_heads = right_dot(low_resid, w_out).astype(jnp.bfloat16)
    dout_all = lax.all_gather(
        grad_heads.reshape(row_count, key_len, width), "keys", axis=1, tiled=True
    ).reshape(row_count, row_len, head_count, HEAD)
    delta_parts = jnp.stack(
        [
            delta_terms(
                contexts[0],
                values[0],
                query_all[0],
                seg_ids[0],
                cumulated_list[0],
                log_sums[0],
                dout_all[0],
            )
        ]
    )
    deltas = lax.psum(delta_parts, "keys")
    row_index = 0
    query_grad, key_grad, value_grad = backward_row(
        contexts[row_index],
        values[row_index],
        query_all[row_index],
        seg_ids[row_index],
        cumulated_list[row_index],
        log_sums[row_index],
        dout_all[row_index],
        deltas[row_index],
    )
    query_parts = [query_grad]
    key_grads = [key_grad]
    value_grads = [value_grad]
    query_own = lax.psum_scatter(
        jnp.stack(query_parts).astype(jnp.bfloat16), "keys", scatter_dimension=1, tiled=True
    ).astype(jnp.float32)
    low_query_grad = query_own.reshape(token_count, width).astype(jnp.bfloat16)
    low_key_grad = jnp.stack(key_grads).reshape(token_count, width).astype(jnp.bfloat16)
    low_value_grad = jnp.stack(value_grads).reshape(token_count, width).astype(jnp.bfloat16)
    grad_query = transpose_dot(low_in, low_query_grad)
    grad_key = transpose_dot(low_in, low_key_grad)
    grad_value = transpose_dot(low_in, low_value_grad)
    grad_norm = (
        right_dot(low_query_grad, w_query)
        + right_dot(low_key_grad, w_key)
        + right_dot(low_value_grad, w_value)
    )
    grad_tokens = (
        (grad_resid + norm_back(grad_norm, unit_in, inverse_in, gain_in))
        .astype(jnp.bfloat16)
        .reshape(row_count, key_len, width)
    )
    norm_grads = jnp.stack(
        [
            jnp.sum(grad_norm * unit_in, 0),
            jnp.sum(grad_norm, 0),
            jnp.sum(grad_mid * unit_mid, 0),
            jnp.sum(grad_mid, 0),
        ],
        1,
    )
    halves = (
        lax.psum_scatter(
            grad_query.astype(jnp.bfloat16), "keys", scatter_dimension=1, tiled=True
        ).astype(jnp.float32),
        lax.psum_scatter(
            grad_key.astype(jnp.bfloat16), "keys", scatter_dimension=1, tiled=True
        ).astype(jnp.float32),
        lax.psum_scatter(
            grad_value.astype(jnp.bfloat16), "keys", scatter_dimension=1, tiled=True
        ).astype(jnp.float32),
        lax.psum_scatter(
            grad_outproj.astype(jnp.bfloat16), "keys", scatter_dimension=1, tiled=True
        ).astype(jnp.float32),
        lax.psum_scatter(
            grad_up.astype(jnp.bfloat16), "keys", scatter_dimension=1, tiled=True
        ).astype(jnp.float32),
        lax.psum_scatter(
            grad_down.astype(jnp.bfloat16), "keys", scatter_dimension=1, tiled=True
        ).astype(jnp.float32),
        lax.psum_scatter(
            norm_grads.astype(jnp.bfloat16), "keys", scatter_dimension=1, tiled=True
        ).astype(jnp.float32),
    )
    reduced = (
        lax.psum_scatter(halves[0], "rows", scatter_dimension=0, tiled=True),
        lax.psum_scatter(halves[1], "rows", scatter_dimension=0, tiled=True),
        lax.psum_scatter(halves[2], "rows", scatter_dimension=0, tiled=True),
        lax.psum_scatter(halves[3], "rows", scatter_dimension=0, tiled=True),
        lax.psum_scatter(halves[4], "rows", scatter_dimension=0, tiled=True),
        lax.psum_scatter(halves[5], "rows", scatter_dimension=0, tiled=True),
        lax.psum_scatter(halves[6], "rows", scatter_dimension=0, tiled=True),
    )
    summed = (
        lax.all_gather(reduced[0].astype(jnp.bfloat16), "keys", axis=1, tiled=True).astype(
            jnp.float32
        ),
        lax.all_gather(reduced[1].astype(jnp.bfloat16), "keys", axis=1, tiled=True).astype(
            jnp.float32
        ),
        lax.all_gather(reduced[2].astype(jnp.bfloat16), "keys", axis=1, tiled=True).astype(
            jnp.float32
        ),
        lax.all_gather(reduced[3].astype(jnp.bfloat16), "keys", axis=1, tiled=True).astype(
            jnp.float32
        ),
        lax.all_gather(reduced[4].astype(jnp.bfloat16), "keys", axis=1, tiled=True).astype(
            jnp.float32
        ),
        lax.all_gather(reduced[5].astype(jnp.bfloat16), "keys", axis=1, tiled=True).astype(
            jnp.float32
        ),
        lax.all_gather(reduced[6].astype(jnp.bfloat16), "keys", axis=1, tiled=True).astype(
            jnp.float32
        ),
    )
    norm_sums = summed[6]
    key_share = jnp.stack(share_list)
    return (
        output.reshape(row_count, key_len, width),
        grad_tokens,
        key_share,
        norm_sums[:, 0],
        norm_sums[:, 1],
        summed[0],
        summed[1],
        summed[2],
        summed[3],
        norm_sums[:, 2],
        norm_sums[:, 3],
        summed[4],
        summed[5],
    )


def solution(mesh):
    in_specs = (
        P("rows", "keys", None),
        P("rows", None),
        P("rows", "keys"),
        P(),
        P(),
        P(),
        P(),
        P(),
        P(),
        P(),
        P(),
        P(),
        P(),
        P("rows", "keys", None),
    )
    out_specs = (
        P("rows", "keys", None),
        P("rows", "keys", None),
        P("rows", "keys"),
        P("rows"),
        P("rows"),
        P("rows", None),
        P("rows", None),
        P("rows", None),
        P("rows", None),
        P("rows"),
        P("rows"),
        P("rows", None),
        P("rows", None),
    )
    return jax.shard_map(body, mesh=mesh, in_specs=in_specs, out_specs=out_specs, check_vma=False)
```

profile of v0, /device:TPU:1, one launch (start us, length us, event | category | flops | bytes accessed | tf_op | source)
XLA Modules:
  0.0 1288.4 jit_solution(8467553058527416649)
XLA Ops:
  10.3 3.1 convolution_convert_fusion.9
  16.8 3.1 convolution_convert_fusion.8
  21.3 4.5 all-gather.6.cloned.1.call-done
  25.8 2.9 copy.66
  28.7 3.9 reshape_squeeze_reshape.4
  36.7 45.9 %while.74 = (s32[]{:T(128)}, f32[512]{0:T(512)S(1)}, f32[512]{0:T(512)S(1)}, f32[512]{0:T(512)S(1)}, f32[2,512,512]{1,2,0:T(8,128)}, /*index=5*/f32[2,12,512]{2,...) while((s32[]{:T(128)}, f32[512]{0:T(512)S(1)}, ...), condition=%wide.region_8.9_spmd.clone, body=%wide.region_2.8_spmd.clone.sunk | while | flops 2046286336 | bytes 120854480 | solution.py:112
  39.0 3.0 broadcast_multiply_fusion.10
  43.1 3.8 convert_reduce_fusion.3
  46.9 3.1 fusion.208
  50.0 7.6 exponential_reduce_fusion.2
  61.9 3.0 broadcast_multiply_fusion.10
  66.0 3.8 convert_reduce_fusion.3
  69.8 3.1 fusion.208
  72.9 7.6 exponential_reduce_fusion.2
  87.3 16.3 %all_gather.34 = f32[2,1,12,1024]{3,1,2,0:T(1,128)S(1)} all-gather(f32[1,1,12,1024]{3,1,2,0:T(1,128)S(1)} %all_gather_stack_reshape.8), channel_id=1, replica_groups=mesh['rows'=16,'keys'=2] {'keys'}, dimensions={0}, use_global_device_ids=true | all-gather | bytes 147456 | tf_op jit(solution)/shard_map/all_gather | solution.py:16
  108.3 26.7 %while.72 = (s32[]{:T(128)}, bf16[2,512,768]{2,1,0:T(8,128)(2,1)}, s32[2,512]{1,0:T(2,128)S(1)}, s32[1,512]{1,0:T(1,128)S(1)}, s32[2]{0:T(128)S(1)}, /*index=5*/...) while((s32[]{:T(128)}, bf16[2,512,768]{2,1,0:T(8,128)(2,1)}, ...), condition=%wide.region_10.11_spmd.clone, body=%wide.region_9.10_spmd.clone.sunk | while | flops 821822464 | bytes 10051769 | solution.py:139
  111.1 8.1 fusion.197
  124.5 8.1 fusion.197
  135.1 10.4 reduce-scatter.28.cloned.1.call-done
  148.6 4.9 fusion.125
  153.5 9.5 fusion.86
  163.1 3.5 multiply_reduce_fusion.1
  170.2 11.1 all-gather.8.cloned.1.call-done
  183.9 3.9 reshape_squeeze_reshape.5
  190.7 20.9 %while.73 = (s32[]{:T(128)}, f32[2,12,512]{2,1,0:T(8,128)S(1)}, s32[2,512]{1,0:T(2,128)S(1)}, s32[1,512]{1,0:T(1,128)S(1)}, s32[2]{0:T(128)S(1)}, /*index=5*/bf1...) while((s32[]{:T(128)}, f32[2,12,512]{2,1,0:T(8,128)S(1)}, ...), condition=%wide.region_18.19_spmd.clone, body=%wide.region_16.18_spmd.clone.sunk | while | flops 824962048 | bytes 44753148 | solution.py:163
  195.4 5.6 multiply_reduce_fusion.7
  205.9 5.6 multiply_reduce_fusion.7
  211.6 4.3 psum.7
  217.1 71.7 %while.75 = (s32[]{:T(128)}, f32[512]{0:T(512)S(1)}, f32[512,12,64]{0,2,1:T(8,128)}, f32[512,12,64]{0,2,1:T(8,128)}, bf16[2,512,768]{2,1,0:T(8,128)(2,1)}, /*ind...) while((s32[]{:T(128)}, f32[512]{0:T(512)S(1)}, ...), condition=%wide.region_23.24_spmd.clone, body=%wide.region_20.23_spmd.clone.sunk | while | flops 3675129856 | bytes 177182640 | solution.py:216
  223.2 4.5 copy-done.2
  227.7 3.6 bitcast_add_fusion.5
  231.3 9.1 fusion.220
  240.5 3.6 fusion.221
  244.1 2.9 fusion.222
  247.0 3.5 bitcast_add_fusion.4
  258.6 4.5 copy-done.2
  263.1 3.6 bitcast_add_fusion.5
  266.7 9.1 fusion.220
  275.9 3.6 fusion.221
  279.5 2.9 fusion.222
  282.5 4.0 bitcast_add_fusion.4
  290.2 3.0 convolution_convert_fusion.2
  309.1 8.6 convolution_convert_fusion
  317.7 6.8 copy.99
  325.8 6.5 convolution_convert_fusion.1
  340.1 3.2 fusion.102
  353.6 10.1 reduce-scatter.56.cloned.1.call-done
  363.8 4.3 copy.100
  368.2 11.7 reduce-scatter.40.cloned.1.call-done
  380.5 9.3 fusion.108
  389.8 116.2 %reduce-scatter.38.cloned.1.call-done = bf16[48,384]{1,0:T(8,128)(2,1)} async-done(((bf16[768,384]{1,0:T(8,128)(2,1)}), bf16[48,384]{1,0:T(8,128)(2,1)}) %reduce-scatter.38.cloned.1.call-update) | async-done | bytes 36880 | tf_op jit(solution)/shard_map/reduce_scatter | solution.py:410
  506.0 4.2 all_gather.41
  514.4 117.4 %reduce-scatter.46.cloned.1.call-done = f32[48,2]{1,0:T(8,128)} async-done(((f32[768,2]{1,0:T(8,128)}), f32[48,2]{1,0:T(8,128)}) %reduce-scatter.46.cloned.1.call-update) | async-done | bytes 400
  632.6 3.8 all-gather.2
  637.0 121.4 %reduce-scatter.34.cloned.1.call-done = bf16[48,384]{1,0:T(8,128)(2,1)} async-done(((bf16[768,384]{1,0:T(8,128)(2,1)}), bf16[48,384]{1,0:T(8,128)(2,1)}) %reduce-scatter.34.cloned.1.call-update) | async-done | bytes 36880 | tf_op jit(solution)/shard_map/reduce_scatter | solution.py:408
  758.3 4.2 all_gather.39
  763.2 121.7 %reduce-scatter.36.cloned.1.call-done = bf16[48,384]{1,0:T(8,128)(2,1)} async-done(((bf16[768,384]{1,0:T(8,128)(2,1)}), bf16[48,384]{1,0:T(8,128)(2,1)}) %reduce-scatter.36.cloned.1.call-update) | async-done | bytes 36880 | tf_op jit(solution)/shard_map/reduce_scatter | solution.py:409
  884.9 4.2 all_gather.40
  889.7 121.5 %reduce-scatter.32.cloned.1.call-done = bf16[48,384]{1,0:T(8,128)(2,1)} async-done(((bf16[768,384]{1,0:T(8,128)(2,1)}), bf16[48,384]{1,0:T(8,128)(2,1)}) %reduce-scatter.32.cloned.1.call-update) | async-done | bytes 36880 | tf_op jit(solution)/shard_map/reduce_scatter | solution.py:407
  1011.2 4.2 all_gather.38
  1016.1 128.3 %reduce-scatter.44.cloned.1.call-done = bf16[192,384]{1,0:T(8,128)(2,1)} async-done(((bf16[3072,384]{1,0:T(8,128)(2,1)}), bf16[192,384]{1,0:T(8,128)(2,1)}) %reduce-scatter.44.cloned.1.call-update) | async-done | bytes 147472 | tf_op jit(solution)/shard_map/reduce_scatter | solution.py:412
  1144.4 4.2 all_gather.43
  1149.4 127.2 %reduce-scatter.42.cloned.1.call-done = bf16[48,1536]{1,0:T(8,128)(2,1)} async-done(((bf16[768,1536]{1,0:T(8,128)(2,1)}), bf16[48,1536]{1,0:T(8,128)(2,1)}) %reduce-scatter.42.cloned.1.call-update) | async-done | bytes 147472 | tf_op jit(solution)/shard_map/reduce_scatter | solution.py:411
  1276.6 4.2 all_gather.42
  (356 shorter events, 121.7 us)
Async XLA Ops:
  7.2 7.5 copy-start
  7.2 3.0 copy-start.14
  7.2 3.0 copy-start.41
  7.2 3.0 copy-start.53
  7.2 18.6 %all-gather.6.cloned.1.call-start = ((), (), s32[]{:S(2)}) async-start(), calls=%async_computation.24 | async-start | bytes 2359296 | tf_op jit(solution)/shard_map/all_gather | solution.py:270
  8.7 8.1 copy-start.35
  10.3 6.5 copy-start.37
  10.3 3.7 copy-start.43
  13.4 132.1 %reduce-scatter.28.cloned.1.call-start = ((), (), s32[]{:S(2)}) async-start(), calls=%async_computation.15 | async-start | bytes 2359296 | tf_op jit(solution)/shard_map/reduce_scatter | solution.py:299
  42.0 4.9 copy-start.1
  50.0 7.7 copy-start.27
  50.0 7.6 copy-start.29
  50.0 7.7 copy-start.3
  50.0 7.7 copy-start.7
  64.9 4.9 copy-start.1
  72.9 7.7 copy-start.27
  72.9 7.6 copy-start.29
  72.9 7.7 copy-start.3
  72.9 7.7 copy-start.7
  135.0 10.4 copy-start.15
  135.0 46.2 %all-gather.8.cloned.1.call-start = ((), (), s32[]{:S(2)}) async-start(), calls=%async_computation.25 | async-start | bytes 2359296 | tf_op jit(solution)/shard_map/all_gather | solution.py:324
  147.8 18.7 %copy-start.17 = (f32[512,768]{1,0:T(8,128)}, f32[512,768]{1,0:T(8,128)S(1)}, u32[]{:S(2)}) copy-start(f32[512,768]{1,0:T(8,128)S(1)} %get-tuple-element.1185) | copy-start | bytes 4718596
  147.9 18.7 %copy-start.39 = (f32[512]{0:T(512)}, f32[512]{0:T(512)S(1)}, u32[]{:S(2)}) copy-start(f32[512]{0:T(512)S(1)} %broadcast_multiply_fusion.6) | copy-start | bytes 6148
  148.6 18.0 %copy-start.44 = (f32[512]{0:T(512)}, f32[512]{0:T(512)S(1)}, u32[]{:S(2)}) copy-start(f32[512]{0:T(512)S(1)} %add_rsqrt_fusion) | copy-start | bytes 6148
  148.6 4.9 copy-start.24
  148.6 14.4 %slice-start = ((s8[4718592]{0:T(1024)(128)(4,1)}), s8[4194304]{0:T(1024)(128)(4,1)S(1)}, s32[]{:S(2)}) async-start(s8[4718592]{0:T(1024)(128)(4,1)} %bitcast.370), calls=%async_computation.32 | async-start | bytes 8388608
  153.5 9.5 copy-start.57
  153.5 9.5 slice-start.1
  163.0 3.5 copy-start.58
  170.1 135.3 %reduce-scatter.30.cloned.1.call-start = ((), (), s32[]{:S(2)}) async-start(), calls=%async_computation.16 | async-start | bytes 2359296 | tf_op jit(solution)/shard_map/reduce_scatter | solution.py:355
  190.7 2.9 copy-start.4
  201.1 2.9 copy-start.4
  218.8 2.5 copy-start.5
  221.3 6.4 copy-start.10
  221.3 6.4 copy-start.21
  223.1 4.5 copy-start.2
  231.3 9.2 copy-start.22
  254.2 2.5 copy-start.5
  256.7 6.4 copy-start.10
  256.7 6.4 copy-start.21
  258.6 4.5 copy-start.2
  266.7 9.2 copy-start.22
  288.9 45.4 %reduce-scatter.54.cloned.1.call-start = ((), (), s32[]{:S(2)}) async-start(), calls=%async_computation.30 | async-start | bytes 1769472
  293.2 2.6 copy-start.6
  295.7 51.2 %reduce-scatter.50.cloned.1.call-start = ((), (), s32[]{:S(2)}) async-start(), calls=%async_computation.28 | async-start | bytes 1769472
  299.2 2.6 copy-start.23
  301.7 47.5 %reduce-scatter.52.cloned.1.call-start = ((), (), s32[]{:S(2)}) async-start(), calls=%async_computation.29 | async-start | bytes 1769472
  305.4 46.1 %reduce-scatter.48.cloned.1.call-start = ((), (), s32[]{:S(2)}) async-start(), calls=%async_computation.27 | async-start | bytes 1769472
  309.0 54.7 %reduce-scatter.56.cloned.1.call-start = ((), (), s32[]{:S(2)}) async-start(), calls=%async_computation.31 | async-start | bytes 7077888
  324.4 55.4 %reduce-scatter.40.cloned.1.call-start = ((), (), s32[]{:S(2)}) async-start(), calls=%async_computation.21 | async-start | bytes 7077888 | tf_op jit(solution)/shard_map/reduce_scatter | solution.py:396
  332.3 4.4 copy-start.26
  332.4 173.7 %reduce-scatter.38.cloned.1.call-start = ((), (), s32[]{:S(2)}) async-start(), calls=%async_computation.20 | async-start | bytes 626688 | tf_op jit(solution)/shard_map/reduce_scatter | solution.py:410
  336.5 295.4 %reduce-scatter.46.cloned.1.call-start = ((), (), s32[]{:S(2)}) async-start(), calls=%async_computation.26 | async-start | bytes 417792
  336.7 2.3 copy-start.51
  336.7 2.3 copy-start.52
  346.9 411.4 %reduce-scatter.34.cloned.1.call-start = ((), (), s32[]{:S(2)}) async-start(), calls=%async_computation.18 | async-start | bytes 626688 | tf_op jit(solution)/shard_map/reduce_scatter | solution.py:408
  349.1 535.7 %reduce-scatter.36.cloned.1.call-start = ((), (), s32[]{:S(2)}) async-start(), calls=%async_computation.19 | async-start | bytes 626688 | tf_op jit(solution)/shard_map/reduce_scatter | solution.py:409
  351.4 659.8 %reduce-scatter.32.cloned.1.call-start = ((), (), s32[]{:S(2)}) async-start(), calls=%async_computation.17 | async-start | bytes 626688 | tf_op jit(solution)/shard_map/reduce_scatter | solution.py:407
  353.6 790.8 %reduce-scatter.44.cloned.1.call-start = ((), (), s32[]{:S(2)}) async-start(), calls=%async_computation.23 | async-start | bytes 2506752 | tf_op jit(solution)/shard_map/reduce_scatter | solution.py:412
  368.1 11.8 copy-start.32
  368.1 11.8 copy-start.34
  368.1 908.5 %reduce-scatter.42.cloned.1.call-start = ((), (), s32[]{:S(2)}) async-start(), calls=%async_computation.22 | async-start | bytes 2506752 | tf_op jit(solution)/shard_map/reduce_scatter | solution.py:411
  380.5 131.1 %copy-start.45 = (f32[512]{0:T(512)S(1)}, f32[512]{0:T(512)}, u32[]{:S(2)}) copy-start(f32[512]{0:T(512)} %get-tuple-element.1044) | copy-start | bytes 6148
  380.5 131.1 %copy-start.13 = (f32[512,768]{1,0:T(8,128)S(1)}, f32[512,768]{1,0:T(8,128)}, u32[]{:S(2)}) copy-start(f32[512,768]{1,0:T(8,128)} %copy-done.11) | copy-start | bytes 4718596
  (29 other events, 34.2 us)
Sparse Core Ops, SparseCore 0:
  13.5 12.2 all-gather.5
  135.2 10.2 reduce-scatter.27
  170.2 10.9 all-gather.7
  289.0 10.2 reduce-scatter.29
  301.3 9.8 reduce-scatter.53
  313.4 9.8 reduce-scatter.49
  325.5 9.8 reduce-scatter.51
  337.8 9.8 reduce-scatter.47
  350.0 13.7 reduce-scatter.55
  366.0 13.7 reduce-scatter.39
  384.5 121.4 reduce-scatter.37
  511.2 120.5 reduce-scatter.45
  637.1 121.2 reduce-scatter.33
  763.6 121.2 reduce-scatter.35
  890.0 121.1 reduce-scatter.31
  1016.7 127.5 reduce-scatter.43
  1149.1 127.4 reduce-scatter.41
where the time goes:
time: 1290 us
  waiting for transfers between devices  902 us (70%)
  matrix products  163 us (13%)
  local copies, waits for them, and re-layouts  106 us (8%)
  blocking collectives  53.8 us (4%)
  other arithmetic  41.4 us (3%)
  between operations  15.6 us (1%)
    reduce_scatter x1, waiting for transfers between devices, body(): lax.psum_scatter(halves[5], 'rows', scatter_dimension=0, tiled=True)  128 us
    unnamed x23, waiting for transfers between devices  128 us
    reduce_scatter x1, waiting for transfers between devices, body(): lax.psum_scatter(halves[4], 'rows', scatter_dimension=0, tiled=True)  127 us
    reduce_scatter x1, waiting for transfers between devices, body(): lax.psum_scatter(halves[2], 'rows', scatter_dimension=0, tiled=True)  122 us
    reduce_scatter x1, waiting for transfers between devices, body(): lax.psum_scatter(halves[0], 'rows', scatter_dimension=0, tiled=True)  122 us
    reduce_scatter x1, waiting for transfers between devices, body(): lax.psum_scatter(halves[1], 'rows', scatter_dimension=0, tiled=True)  121 us
    reduce_scatter x1, waiting for transfers between devices, body(): lax.psum_scatter(halves[3], 'rows', scatter_dimension=0, tiled=True)  116 us
    unnamed x110, local copies, waits for them, and re-layouts  46 us
  transfers between devices with their start and end apart: 17, of which 12 were waited for; matrix products, arithmetic and copies ran while one was open for 7% of the time, Pallas kernels for 0%

commit v1 on v0

--- a/solution.py
+++ b/solution.py
@@ -1,6 +1,10 @@
+import functools
+
 import jax
 import jax.numpy as jnp
 from jax import lax
+from jax.experimental import pallas as pl
+from jax.experimental.pallas import tpu as pltpu
 from jax.sharding import PartitionSpec as P
 
 HEAD = 64
@@ -227,7 +231,197 @@
     return (maxima, totals)
 
 
+MESH = pl.DeviceIdType.MESH
+
+
+def grid_of(rows):
+    short = round((rows / 2) ** (1 / 3))
+    return (2 * short, short, short) if 2 * short**3 == rows else (rows, 1, 1)
+
+
+def place(grid):
+    _, wide, deep = grid
+    me, core = lax.axis_index("rows"), lax.axis_index("keys")
+    slow, mid, fast = me // (wide * deep), (me // deep) % wide, me % deep
+    return slow, fast + core * (mid - fast), mid + core * (fast - mid), core
+
+
+def rank_of(grid, slow, first, second, core):
+    mid, fast = second + core * (first - second), first + core * (second - first)
+    return (slow * grid[1] + mid) * grid[2] + fast
+
+
+def reduce_kernel(grid, count, *refs):
+    parts, refs = refs[:count], refs[count:]
+    outs, refs = refs[:count], refs[count:]
+    got1, refs = refs[:count], refs[count:]
+    sum1, refs = refs[:count], refs[count:]
+    got2, refs = refs[:count], refs[count:]
+    sum2, refs = refs[:count], refs[count:]
+    got3, refs = refs[:count], refs[count:]
+    mine, refs = refs[:count], refs[count:]
+    pair, refs = refs[:count], refs[count:]
+    send1, recv1, send2, recv2, send3, recv3, send4, recv4 = refs
+    long, wide, deep = grid
+    slow, first, second, core = place(grid)
+
+    def peers(size, here, target):
+        return [target(lax.rem(here + step, size)) for step in range(1, size)]
+
+    near = peers(wide, first, lambda p: (p, rank_of(grid, slow, p, second, core)))
+    next_ = peers(deep, second, lambda p: (p, rank_of(grid, slow, first, p, core)))
+    far = peers(long, slow, lambda p: (p, rank_of(grid, p, first, second, core)))
+    me = rank_of(grid, slow, first, second, core)
+    other = 1 - core
+
+    barrier = pltpu.get_barrier_semaphore()
+    for _, rank in near + next_ + far:
+        pl.semaphore_signal(barrier, inc=1, device_id=(rank, core), device_id_type=MESH)
+    pl.semaphore_signal(barrier, inc=1, device_id=(me, other), device_id_type=MESH)
+    pl.semaphore_wait(barrier, len(near) + len(next_) + len(far) + 1)
+
+    def copy(source, target, send, recv, device):
+        return pltpu.make_async_remote_copy(
+            src_ref=source,
+            dst_ref=target,
+            send_sem=send,
+            recv_sem=recv,
+            device_id=device,
+            device_id_type=MESH,
+        )
+
+    first_copies = [
+        [
+            copy(
+                parts[j].at[:, p], got1[j].at[i], send1.at[j, i], recv1.at[j, i], (rank, core)
+            )
+            for i, (p, rank) in enumerate(near)
+        ]
+        for j in range(count)
+    ]
+    for group in first_copies:
+        for one in group:
+            one.start()
+    second_copies = []
+    for j in range(count):
+        for one in first_copies[j]:
+            one.wait_recv()
+
+        @pl.loop(0, long * deep)
+        def _(step, j=j):
+            a, b = step // deep, step % deep
+            total = parts[j][a, first, b].astype(jnp.float32)
+            for i in range(len(near)):
+                total = total + got1[j][i, a, b].astype(jnp.float32)
+            sum1[j][a, b] = total.astype(sum1[j].dtype)
+
+        group = [
+            copy(sum1[j].at[:, p], got2[j].at[i], send2.at[j, i], recv2.at[j, i], (rank, core))
+            for i, (p, rank) in enumerate(next_)
+        ]
+        for one in group:
+            one.start()
+        second_copies.append(group)
+    third_copies = []
+    for j in range(count):
+        for one in second_copies[j]:
+            one.wait_recv()
+
+        @pl.loop(0, long)
+        def _(a, j=j):
+            total = sum1[j][a, second].astype(jnp.float32)
+            for i in range(len(next_)):
+                total = total + got2[j][i, a].astype(jnp.float32)
+            sum2[j][a] = total.astype(sum2[j].dtype)
+
+        group = [
+            copy(sum2[j].at[p], got3[j].at[i], send3.at[j, i], recv3.at[j, i], (rank, core))
+            for i, (p, rank) in enumerate(far)
+        ]
+        for one in group:
+            one.start()
+        third_copies.append(group)
+    last_copies = []
+    for j in range(count):
+        for one in third_copies[j]:
+            one.wait_recv()
+        total = sum2[j][slow].astype(jnp.float32)
+        for i in range(len(far)):
+            total = total + got3[j][i].astype(jnp.float32)
+        mine[j][...] = total.astype(mine[j].dtype)
+        one = copy(mine[j], pair[j], send4.at[j], recv4.at[j], (me, other))
+        one.start()
+        last_copies.append(one)
+    for j in range(count):
+        last_copies[j].wait_recv()
+        own, their = mine[j][...].astype(jnp.float32), pair[j][...].astype(jnp.float32)
+        height, width = own.shape
+        if j == count - 1:
+            outs[j][...] = own + their
+        else:
+            outs[j][:, pl.ds(pl.multiple_of(core * width, 128), width)] = own
+            outs[j][:, pl.ds(pl.multiple_of(other * width, 128), width)] = their
+    for group in first_copies + second_copies + third_copies + [last_copies]:
+        for one in group:
+            one.wait_send()
+
+
+def reduce_rows(halves, norm_grads, rows):
+    grid = grid_of(rows)
+    long, wide, deep = grid
+    core = lax.axis_index("keys")
+    parts, heights = [], []
+    for half in halves:
+        height = half.shape[0] // rows
+        padded = -(-height // 16) * 16
+        part = half.reshape(rows, height, half.shape[1])
+        parts.append(jnp.pad(part, ((0, 0), (0, padded - height), (0, 0))))
+        heights.append(height)
+    vectors = norm_grads.reshape(rows, -1, 4).transpose(0, 2, 1)
+    span = vectors.shape[2]
+    parts.append(jnp.pad(vectors, ((0, 0), (0, 4), (0, 128 - span))))
+    count = len(parts)
+    blocks = [part.shape[1:] for part in parts]
+    ordered = []
+    for part, block in zip(parts, blocks):
+        cube = part.reshape((long, wide, deep) + block)
+        ordered.append(jnp.where(core == 0, cube.swapaxes(1, 2), cube))
+    scratch = []
+    dtypes = [part.dtype for part in parts]
+    for lead in (
+        (max(wide - 1, 1), long, deep),
+        (long, deep),
+        (max(deep - 1, 1), long),
+        (long,),
+        (max(long - 1, 1),),
+        (),
+        (),
+    ):
+        scratch += [pltpu.VMEM(lead + block, kind) for block, kind in zip(blocks, dtypes)]
+    for peers in (wide - 1, deep - 1, long - 1):
+        scratch += [pltpu.SemaphoreType.DMA((count, max(peers, 1)))] * 2
+    scratch += [pltpu.SemaphoreType.DMA((count,))] * 2
+    out_shape = [
+        jax.ShapeDtypeStruct((block[0], block[1] * (1 if j == count - 1 else 2)), jnp.float32)
+        for j, block in enumerate(blocks)
+    ]
+    results = pl.pallas_call(
+        functools.partial(reduce_kernel, grid, count),
+        out_shape=out_shape,
+        in_specs=[pl.BlockSpec(memory_space=pltpu.VMEM)] * count,
+        out_specs=[pl.BlockSpec(memory_space=pltpu.VMEM)] * count,
+        scratch_shapes=scratch,
+        compiler_params=pltpu.CompilerParams(
+            collective_id=0, has_side_effects=True, vmem_limit_bytes=60 * 1024 * 1024
+        ),
+        name="reduce_rows",
+    )(*ordered)
+    summed = [result[:height] for result, height in zip(results, heights)]
+    return summed, results[-1][:4, :span].T
+
+
 def body(
+    rows,
     tokens,
     seg_ids,
     doc_starts,
@@ -383,59 +577,18 @@
     halves = (
         lax.psum_scatter(
             grad_query.astype(jnp.bfloat16), "keys", scatter_dimension=1, tiled=True
-        ).astype(jnp.float32),
-        lax.psum_scatter(
-            grad_key.astype(jnp.bfloat16), "keys", scatter_dimension=1, tiled=True
-        ).astype(jnp.float32),
+        ),
+        lax.psum_scatter(grad_key.astype(jnp.bfloat16), "keys", scatter_dimension=1, tiled=True),
         lax.psum_scatter(
             grad_value.astype(jnp.bfloat16), "keys", scatter_dimension=1, tiled=True
-        ).astype(jnp.float32),
+        ),
         lax.psum_scatter(
             grad_outproj.astype(jnp.bfloat16), "keys", scatter_dimension=1, tiled=True
-        ).astype(jnp.float32),
-        lax.psum_scatter(
-            grad_up.astype(jnp.bfloat16), "keys", scatter_dimension=1, tiled=True
-        ).astype(jnp.float32),
-        lax.psum_scatter(
-            grad_down.astype(jnp.bfloat16), "keys", scatter_dimension=1, tiled=True
-        ).astype(jnp.float32),
-        lax.psum_scatter(
-            norm_grads.astype(jnp.bfloat16), "keys", scatter_dimension=1, tiled=True
-        ).astype(jnp.float32),
-    )
-    reduced = (
-        lax.psum_scatter(halves[0], "rows", scatter_dimension=0, tiled=True),
-        lax.psum_scatter(halves[1], "rows", scatter_dimension=0, tiled=True),
-        lax.psum_scatter(halves[2], "rows", scatter_dimension=0, tiled=True),
-        lax.psum_scatter(halves[3], "rows", scatter_dimension=0, tiled=True),
-        lax.psum_scatter(halves[4], "rows", scatter_dimension=0, tiled=True),
-        lax.psum_scatter(halves[5], "rows", scatter_dimension=0, tiled=True),
-        lax.psum_scatter(halves[6], "rows", scatter_dimension=0, tiled=True),
-    )
-    summed = (
-        lax.all_gather(reduced[0].astype(jnp.bfloat16), "keys", axis=1, tiled=True).astype(
-            jnp.float32
         ),
-        lax.all_gather(reduced[1].astype(jnp.bfloat16), "keys", axis=1, tiled=True).astype(
-            jnp.float32
-        ),
-        lax.all_gather(reduced[2].astype(jnp.bfloat16), "keys", axis=1, tiled=True).astype(
-            jnp.float32
-        ),
-        lax.all_gather(reduced[3].astype(jnp.bfloat16), "keys", axis=1, tiled=True).astype(
-            jnp.float32
-        ),
-        lax.all_gather(reduced[4].astype(jnp.bfloat16), "keys", axis=1, tiled=True).astype(
-            jnp.float32
-        ),
-        lax.all_gather(reduced[5].astype(jnp.bfloat16), "keys", axis=1, tiled=True).astype(
-            jnp.float32
-        ),
-        lax.all_gather(reduced[6].astype(jnp.bfloat16), "keys", axis=1, tiled=True).astype(
-            jnp.float32
-        ),
-    )
-    norm_sums = summed[6]
+        lax.psum_scatter(grad_up.astype(jnp.bfloat16), "keys", scatter_dimension=1, tiled=True),
+        lax.psum_scatter(grad_down.astype(jnp.bfloat16), "keys", scatter_dimension=1, tiled=True),
+    )
+    summed, norm_sums = reduce_rows(halves, norm_grads, rows)
     key_share = jnp.stack(share_list)
     return (
         output.reshape(row_count, key_len, width),
@@ -486,4 +639,6 @@
         P("rows", None),
         P("rows", None),
     )
-    return jax.shard_map(body, mesh=mesh, in_specs=in_specs, out_specs=out_specs, check_vma=False)
+    return jax.shard_map(
+        functools.partial(body, mesh.shape["rows"]), mesh=mesh, in_specs=in_specs, out_specs=out_specs, check_vma=False
+    )

time: 1290 us -> 495 us (0.38)
  waiting for transfers between devices: 902 us -> 31.8 us
  Pallas kernels: 0 us -> 103 us
  blocking collectives: 53.8 us -> 8.54 us
    reduce_scatter x6 -> x0, waiting for transfers between devices: 736 us -> none  [the longest x1 128 us: body(): lax.psum_scatter(halves[5], 'rows', scatter_dimension=0, tiled=True)]
    unnamed x23 -> x15, waiting for transfers between devices: 128 us -> 0.19 us
    pallas_call x0 -> x1, Pallas kernels: none -> 103 us  [reduce_rows(): pl.pallas_call(functools.partial(reduce_kernel, grid, count), out_shape=o...]
    all_gather x7 -> x0, blocking collectives: 28.8 us -> none  [the longest x1 4.18 us: body(): lax.all_gather(reduced[0].astype(jnp.bfloat16), 'keys', axis=1, tiled=True)]
    all_gather x2, blocking collectives: 18.2 us -> 4.28 us  [joined(): pieces = jax.tree.map(lambda part: lax.all_gather(part, axis), value)]
    unnamed x110 -> x117, local copies, waits for them, and re-layouts: 46 us -> 48.2 us
  transfers between devices with their start and end apart: 17 -> 10, of which waited for: 12 -> 4; matrix products, arithmetic and copies ran while one was open for 7% -> 18% of each run, Pallas kernels for 0% -> 0%
where the time goes in v1:
time: 495 us; the launch traced here: 489 us
  matrix products  162 us (33%)
  local copies, waits for them, and re-layouts  114 us (23%)
  Pallas kernels  103 us (21%)
  other arithmetic  47.7 us (10%)
  waiting for transfers between devices  31.8 us (6%)
  between operations  15.1 us (3%)
  blocking collectives  8.54 us (2%)
  loops' own time  6.24 us (1%)
    pallas_call x1, Pallas kernels, reduce_rows(): pl.pallas_call(functools.partial(reduce_kernel, grid, count), out_shape=o...  103 us
    unnamed x117, local copies, waits for them, and re-layouts  48.2 us
    dot_general x4, matrix products, scan_step(): jnp.einsum('qhd,khd->hqk', dout_blk, values, preferred_element_type=jnp.f...  29.6 us
    dot_general x6, matrix products, transpose_dot(): jnp.einsum('ti,to->io', left, right, preferred_element_type=jnp.float32)  23.6 us
    dot_general x6, matrix products, right_dot(): jnp.einsum('ti,oi->to', left, right, preferred_element_type=jnp.float32)  20.7 us
    dot_general x2, matrix products, scan_step(): jnp.einsum('hqk,khd->qhd', weights, values, preferred_element_type=jnp.fl...  16.3 us
    reduce_sum x2, other arithmetic, scan_step(): totals = jnp.sum(jnp.exp(logits - maxima[..., None]), -1)  15.2 us
    dot_general x6, matrix products, block_scores(): jnp.einsum('qhd,khd->hqk', query_blk, key_vecs, preferred_element_type=jn...  13.3 us
  transfers between devices with their start and end apart: 10, of which 4 were waited for; matrix products, arithmetic and copies ran while one was open for 18% of the time, Pallas kernels for 0%

profile of v1, /device:TPU:1, one launch (start us, length us, event | category | flops | bytes accessed | tf_op | source)
XLA Modules:
  0.0 489.3 jit_solution(451467421835590339)
XLA Ops:
  10.3 3.1 convolution_convert_fusion.9
  16.8 3.1 convolution_convert_fusion.8
  21.3 4.5 all-gather.5.cloned.1.call-done
  25.8 2.9 copy.80
  28.7 3.9 reshape_squeeze_reshape.4
  32.6 2.9 copy.88
  36.7 46.0 %while.74 = (s32[]{:T(128)}, f32[512]{0:T(512)S(1)}, f32[512]{0:T(512)S(1)}, f32[512]{0:T(512)S(1)}, f32[2,512,512]{1,2,0:T(8,128)}, /*index=5*/f32[2,12,512]{2,...) while((s32[]{:T(128)}, f32[512]{0:T(512)S(1)}, ...), condition=%wide.region_8.9_spmd.clone, body=%wide.region_2.8_spmd.clone.sunk | while | flops 2046286336 | bytes 120854480 | solution.py:116
  39.0 3.0 broadcast_multiply_fusion.10
  43.1 3.8 convert_reduce_fusion.3
  46.9 3.1 fusion.208
  50.0 7.6 %exponential_reduce_fusion.2 = f32[12,512]{1,0:T(8,128)S(1)} fusion(f32[12,512,512]{1,2,0:T(8,128)} %copy-done.1, f32[12,512]{1,0:T(8,128)S(1)} %fusion.208, f32[512,512]{0,1:T(8,128)} %bitcast.348, pred[512,512]{0,1:T(8,128)(4,1)} %compare_and_fusion.12), kind=kLoop, calls=%fused_computation.37.clone.1 | loop fusion | flops 12576768 | bytes 13942784 | tf_op jit(solution)/shard_map/while/body/eval_jaxpr/reduce_sum | solution.py:108
  62.0 3.0 broadcast_multiply_fusion.10
  66.0 3.8 convert_reduce_fusion.3
  69.8 3.1 fusion.208
  73.0 7.6 %exponential_reduce_fusion.2 = f32[12,512]{1,0:T(8,128)S(1)} fusion(f32[12,512,512]{1,2,0:T(8,128)} %copy-done.1, f32[12,512]{1,0:T(8,128)S(1)} %fusion.208, f32[512,512]{0,1:T(8,128)} %bitcast.348, pred[512,512]{0,1:T(8,128)(4,1)} %compare_and_fusion.12), kind=kLoop, calls=%fused_computation.37.clone.1 | loop fusion | flops 12576768 | bytes 13942784 | tf_op jit(solution)/shard_map/while/body/eval_jaxpr/reduce_sum | solution.py:108
  85.2 1.9 all_gather.14
  87.4 2.4 all_gather.13
  90.3 2.9 copy.89
  94.5 26.7 %while.72 = (s32[]{:T(128)}, bf16[2,512,768]{2,1,0:T(8,128)(2,1)}, s32[2,512]{1,0:T(2,128)S(1)}, s32[1,512]{1,0:T(1,128)S(1)}, s32[2]{0:T(128)S(1)}, /*index=5*/...) while((s32[]{:T(128)}, bf16[2,512,768]{2,1,0:T(8,128)(2,1)}, ...), condition=%wide.region_10.11_spmd.clone, body=%wide.region_9.10_spmd.clone.sunk | while | flops 821822464 | bytes 10051769 | solution.py:143
  97.3 8.1 %fusion.197 = bf16[12,512,64]{1,2,0:T(8,128)(2,1)} fusion(bf16[512,12,64]{0,2,1:T(8,128)(2,1)} %get-tuple-element.1669, f32[12,512]{1,0:T(8,128)S(1)} %dynamic-slice_bitcast_fusion.13, f32[512,512]{1,0:T(8,128)S(1)} %dynamic-slice_bitcast_fusion.14, pred[512,512]{1,0:T(8,128)(4,1)S(1)} %compare_and_fusion.10, ...), kind=kOutput, calls=%fused_computation.7.clone.1 | convolution fusion | flops 821035008 | bytes 4481028 | tf_op jit(solution)/shard_map/while/body/eval_jaxpr/hqk,khd->qhd/dot_general | solution.py:136
  110.7 8.1 %fusion.197 = bf16[12,512,64]{1,2,0:T(8,128)(2,1)} fusion(bf16[512,12,64]{0,2,1:T(8,128)(2,1)} %get-tuple-element.1669, f32[12,512]{1,0:T(8,128)S(1)} %dynamic-slice_bitcast_fusion.13, f32[512,512]{1,0:T(8,128)S(1)} %dynamic-slice_bitcast_fusion.14, pred[512,512]{1,0:T(8,128)(4,1)S(1)} %compare_and_fusion.10, ...), kind=kOutput, calls=%fused_computation.7.clone.1 | convolution fusion | flops 821035008 | bytes 4481028 | tf_op jit(solution)/shard_map/while/body/eval_jaxpr/hqk,khd->qhd/dot_general | solution.py:136
  121.5 10.2 %reduce-scatter.19.cloned.1.call-done = bf16[1,512,768]{2,1,0:T(8,128)(2,1)} async-done(((bf16[1,1024,768]{2,1,0:T(8,128)(2,1)}), bf16[1,512,768]{2,1,0:T(8,128)(2,1)}) %reduce-scatter.19.cloned.1.call-update) | async-done | bytes 786448 | tf_op jit(solution)/shard_map/reduce_scatter | solution.py:493
  131.6 2.4 fusion.136
  134.8 4.9 fusion.125
  139.7 9.5 %fusion.86 = bf16[512,3072]{1,0:T(8,128)(2,1)S(1)} fusion(f32[512,3072]{1,0:T(8,128)S(1)} %fusion.125, bf16[3072,768]{1,0:T(8,128)(2,1)} %param.36, bf16[1,512,768]{2,1,0:T(8,128)(2,1)S(1)} %copy-done.25), kind=kOutput, calls=%fused_computation.126 | convolution fusion | flops 2447376384 | bytes 14942208 | tf_op jit(solution)/shard_map/ti,oi->to/dot_general | solution.py:52
  149.2 3.6 multiply_reduce_fusion.1
  156.4 11.1 %all-gather.7.cloned.1.call-done = bf16[1024,768]{1,0:T(8,128)(2,1)} async-done(((bf16[512,768]{1,0:T(8,128)(2,1)}), bf16[1024,768]{1,0:T(8,128)(2,1)}) %all-gather.7.cloned.1.call-update) | async-done | bytes 1572880 | tf_op jit(solution)/shard_map/all_gather | solution.py:518
  167.4 2.6 copy.92
  170.1 3.8 reshape_squeeze_reshape.5
  173.9 2.9 copy.99
  176.8 20.9 %while.73 = (s32[]{:T(128)}, f32[2,12,512]{2,1,0:T(8,128)S(1)}, s32[2,512]{1,0:T(2,128)S(1)}, s32[1,512]{1,0:T(1,128)S(1)}, s32[2]{0:T(128)S(1)}, /*index=5*/bf1...) while((s32[]{:T(128)}, f32[2,12,512]{2,1,0:T(8,128)S(1)}, ...), condition=%wide.region_18.19_spmd.clone, body=%wide.region_16.18_spmd.clone.sunk | while | flops 824962048 | bytes 44753148 | solution.py:167
  181.6 5.6 %multiply_reduce_fusion.7 = f32[12,512]{1,0:T(8,128)S(1)} fusion(f32[12,512,512]{1,2,0:T(8,128)S(1)} %fusion.202, f32[12,512]{1,0:T(8,128)S(1)} %dynamic-slice_bitcast_fusion.15, f32[512,512]{0,1:T(8,128)S(1)} %dynamic-slice_bitcast_fusion.16, pred[512,512]{0,1:T(8,128)(4,1)S(1)} %compare_and_fusion.11, ...), kind=kOutput, calls=%fused_computation.22.clone.1 | convolution fusion | flops 421521408 | bytes 15523844 | tf_op jit(solution)/shard_map/while/body/eval_jaxpr/qhd,khd->hqk/dot_general | solution.py:157
  192.0 5.6 %multiply_reduce_fusion.7 = f32[12,512]{1,0:T(8,128)S(1)} fusion(f32[12,512,512]{1,2,0:T(8,128)S(1)} %fusion.202, f32[12,512]{1,0:T(8,128)S(1)} %dynamic-slice_bitcast_fusion.15, f32[512,512]{0,1:T(8,128)S(1)} %dynamic-slice_bitcast_fusion.16, pred[512,512]{0,1:T(8,128)(4,1)S(1)} %compare_and_fusion.11, ...), kind=kOutput, calls=%fused_computation.22.clone.1 | convolution fusion | flops 421521408 | bytes 15523844 | tf_op jit(solution)/shard_map/while/body/eval_jaxpr/qhd,khd->hqk/dot_general | solution.py:157
  197.7 4.3 psum.7
  203.3 71.7 %while.75 = (s32[]{:T(128)}, f32[512]{0:T(512)S(1)}, f32[512,12,64]{0,2,1:T(8,128)}, f32[512,12,64]{0,2,1:T(8,128)}, bf16[2,512,768]{2,1,0:T(8,128)(2,1)}, /*ind...) while((s32[]{:T(128)}, f32[512]{0:T(512)S(1)}, ...), condition=%wide.region_23.24_spmd.clone, body=%wide.region_20.23_spmd.clone.sunk | while | flops 3675129856 | bytes 177182640 | solution.py:220
  207.3 1.8 broadcast_multiply_fusion.11
  209.2 4.5 copy-done.2
  213.7 3.6 bitcast_add_fusion.5
  217.4 9.1 %fusion.220 = (f32[512,512]{1,0:T(8,128)S(1)}, f32[512]{0:T(512)S(1)}, f32[12,512,512]{2,1,0:T(8,128)S(1)}) fusion(f32[12,512]{1,0:T(8,128)S(1)} %get-tuple-element.1571, bf16[512,12,64]{0,2,1:T(8,128)(2,1)} %get-tuple-element.1770, bf16[2,512,12,64]{1,3,2,0:T(8,128)(2,1)S(1)} %copy-done.10, s32[]{:T(128)S(6)} %sub.491, ...), kind=kOutput, calls=%fused_computation.218.clone.1 | convolution fusion | flops 424410624 | bytes 29165572 | tf_op jit(solution)/shard_map/while/body/eval_jaxpr/qhd,khd->hqk/dot_general | solution.py:184
  226.5 3.6 fusion.221
  230.2 2.9 fusion.222
  233.1 3.5 bitcast_add_fusion.4
  244.7 4.5 copy-done.2
  249.2 3.6 bitcast_add_fusion.5
  252.9 9.1 %fusion.220 = (f32[512,512]{1,0:T(8,128)S(1)}, f32[512]{0:T(512)S(1)}, f32[12,512,512]{2,1,0:T(8,128)S(1)}) fusion(f32[12,512]{1,0:T(8,128)S(1)} %get-tuple-element.1571, bf16[512,12,64]{0,2,1:T(8,128)(2,1)} %get-tuple-element.1770, bf16[2,512,12,64]{1,3,2,0:T(8,128)(2,1)S(1)} %copy-done.10, s32[]{:T(128)S(6)} %sub.491, ...), kind=kOutput, calls=%fused_computation.218.clone.1 | convolution fusion | flops 424410624 | bytes 29165572 | tf_op jit(solution)/shard_map/while/body/eval_jaxpr/qhd,khd->hqk/dot_general | solution.py:184
  262.0 3.6 fusion.221
  265.7 2.9 fusion.222
  268.6 4.0 bitcast_add_fusion.4
  276.4 3.0 convolution_convert_fusion.2
  279.4 2.5 copy.116
  283.2 2.2 convolution_convert_fusion.4
  285.4 2.5 copy.112
  291.6 2.1 convolution_convert_fusion.5
  295.3 8.7 %convolution_convert_fusion = bf16[3072,768]{1,0:T(8,128)(2,1)} fusion(bf16[1,512,768]{2,1,0:T(8,128)(2,1)} %param.37, f32[512,3072]{1,0:T(8,128)} %copy-done.59), kind=kOutput, calls=%fused_computation.128 | convolution fusion | flops 2432434176 | bytes 11796480 | tf_op jit(solution)/shard_map/ti,to->io/dot_general | solution.py:48
  304.0 6.7 %copy.118 = bf16[3072,768]{0,1:T(8,128)(2,1)} copy(bf16[3072,768]{1,0:T(8,128)(2,1)} %convolution_convert_fusion) | data formatting | bytes 9437184
  312.1 6.6 %convolution_convert_fusion.1 = bf16[768,3072]{1,0:T(8,128)(2,1)} fusion(bf16[512,3072]{1,0:T(8,128)(2,1)} %copy-done.60, f32[512,768]{1,0:T(8,128)S(1)} %copy-done.18, f32[768]{0:T(1024)} %param.34, f32[768]{0:T(1024)} %param.33, f32[512]{0:T(512)S(1)} %copy-done.49, f32[512]{0:T(512)S(1)} %copy-done.43), kind=kOutput, calls=%fused_computation.129 | convolution fusion | flops 2420244480 | bytes 9447424 | tf_op jit(solution)/shard_map/ti,to->io/dot_general | solution.py:48
  322.1 8.9 %fusion.108 = bf16[1,512,768]{2,1,0:T(8,128)(2,1)} fusion(f32[512,768]{1,0:T(8,128)S(1)} %copy-done.18, bf16[3072,768]{1,0:T(8,128)(2,1)} %param.36, f32[512,3072]{1,0:T(8,128)} %copy-done.59), kind=kOutput, calls=%fused_computation.174 | convolution fusion | flops 2430861312 | bytes 13369344 | tf_op jit(solution)/shard_map/dot_general | solution.py:502
  331.0 2.0 fusion.137
  341.6 3.2 fusion.102
  350.4 2.8 fusion.110
  355.5 3.0 copy.119
  360.1 5.8 %reduce-scatter.23.cloned.1.call-done = bf16[768,1536]{1,0:T(8,128)(2,1)} async-done(((bf16[768,3072]{1,0:T(8,128)(2,1)}), bf16[768,1536]{1,0:T(8,128)(2,1)}) %reduce-scatter.23.cloned.1.call-update) | async-done | bytes 2359312 | tf_op jit(solution)/shard_map/reduce_scatter | solution.py:588
  366.0 4.0 copy_select_fusion.1.refs_4_
  370.0 102.9 %reduce_rows.1 = (f32[48,768]{1,0:T(8,128)}, f32[48,768]{1,0:T(8,128)}, f32[48,768]{1,0:T(8,128)}, f32[48,768]{1,0:T(8,128)}, f32[48,3072]{1,0:T(8,128)}, /*index=5*/f32[192,768]{1,0:T(8,128)}, f32[8,128]{1,0:T(8,128)}) custom-call(bf16[4,2,2,48,384]{4,3,2,1,0:T(8,128)(2,1)} %copy_select_fusion.5.refs_0_, ...), custom_call_target="tpu_custom_call" | custom-call | tf_op jit(solution)/shard_map/reduce_rows/pallas_call | solution.py:408
  (335 shorter events, 99.0 us)
Async XLA Ops:
  7.2 7.5 %copy-start = (bf16[768,768]{1,0:T(8,128)(2,1)S(1)}, bf16[768,768]{1,0:T(8,128)(2,1)}, u32[]{:S(2)}) copy-start(bf16[768,768]{1,0:T(8,128)(2,1)} %param.31) | copy-start | bytes 3538948
  7.2 3.0 copy-start.14
  7.2 3.0 copy-start.44
  7.2 3.0 copy-start.56
  7.2 18.6 %all-gather.5.cloned.1.call-start = ((), (), s32[]{:S(2)}) async-start(), calls=%async_computation.11 | async-start | bytes 2359296 | tf_op jit(solution)/shard_map/all_gather | solution.py:464
  8.7 8.1 %copy-start.38 = (f32[512]{0:T(512)}, f32[512]{0:T(512)S(1)}, u32[]{:S(2)}) copy-start(f32[512]{0:T(512)S(1)} %broadcast_multiply_fusion.7) | copy-start | bytes 6148
  10.3 6.5 %copy-start.40 = (f32[512]{0:T(512)}, f32[512]{0:T(512)S(1)}, u32[]{:S(2)}) copy-start(f32[512]{0:T(512)S(1)} %add_rsqrt_fusion.1) | copy-start | bytes 6148
  10.3 3.7 copy-start.47
  13.4 118.2 %reduce-scatter.19.cloned.1.call-start = ((), (), s32[]{:S(2)}) async-start(), calls=%async_computation.8 | async-start | bytes 2359296 | tf_op jit(solution)/shard_map/reduce_scatter | solution.py:493
  19.9 1.4 copy-start.51
  42.0 4.9 copy-start.1
  50.0 7.7 %copy-start.30 = (f32[2,12,512]{2,1,0:T(8,128)S(1)}, f32[2,12,512]{2,1,0:T(8,128)}, u32[]{:S(2)}) copy-start(f32[2,12,512]{2,1,0:T(8,128)} %get-tuple-element.1604) | copy-start | bytes 147460 | tf_op jit(solution)/shard_map/while
  50.0 7.6 %copy-start.32 = (f32[2,12,512]{2,1,0:T(8,128)S(1)}, f32[2,12,512]{2,1,0:T(8,128)}, u32[]{:S(2)}) copy-start(f32[2,12,512]{2,1,0:T(8,128)} %get-tuple-element.1603) | copy-start | bytes 147460 | tf_op jit(solution)/shard_map/while
  50.0 7.7 %copy-start.3 = (f32[512,512]{1,0:T(8,128)S(1)}, f32[512,512]{1,0:T(8,128)}, u32[]{:S(2)}) copy-start(f32[512,512]{1,0:T(8,128)} %get-tuple-element.1551) | copy-start | bytes 3145732 | tf_op jit(solution)/shard_map/while
  50.0 7.7 %copy-start.7 = (f32[2,512,512]{1,2,0:T(8,128)S(1)}, f32[2,512,512]{1,2,0:T(8,128)}, u32[]{:S(2)}) copy-start(f32[2,512,512]{1,2,0:T(8,128)} %get-tuple-element.1602) | copy-start | bytes 6291460 | tf_op jit(solution)/shard_map/while
  65.0 4.9 copy-start.1
  72.9 7.7 %copy-start.30 = (f32[2,12,512]{2,1,0:T(8,128)S(1)}, f32[2,12,512]{2,1,0:T(8,128)}, u32[]{:S(2)}) copy-start(f32[2,12,512]{2,1,0:T(8,128)} %get-tuple-element.1604) | copy-start | bytes 147460 | tf_op jit(solution)/shard_map/while
  72.9 7.6 %copy-start.32 = (f32[2,12,512]{2,1,0:T(8,128)S(1)}, f32[2,12,512]{2,1,0:T(8,128)}, u32[]{:S(2)}) copy-start(f32[2,12,512]{2,1,0:T(8,128)} %get-tuple-element.1603) | copy-start | bytes 147460 | tf_op jit(solution)/shard_map/while
  73.0 7.7 %copy-start.3 = (f32[512,512]{1,0:T(8,128)S(1)}, f32[512,512]{1,0:T(8,128)}, u32[]{:S(2)}) copy-start(f32[512,512]{1,0:T(8,128)} %get-tuple-element.1551) | copy-start | bytes 3145732 | tf_op jit(solution)/shard_map/while
  73.0 7.7 %copy-start.7 = (f32[2,512,512]{1,2,0:T(8,128)S(1)}, f32[2,512,512]{1,2,0:T(8,128)}, u32[]{:S(2)}) copy-start(f32[2,512,512]{1,2,0:T(8,128)} %get-tuple-element.1602) | copy-start | bytes 6291460 | tf_op jit(solution)/shard_map/while
  121.2 10.4 %copy-start.15 = (bf16[1,512,768]{2,1,0:T(8,128)(2,1)S(1)}, bf16[1,512,768]{2,1,0:T(8,128)(2,1)}, u32[]{:S(2)}) copy-start(bf16[1,512,768]{2,1,0:T(8,128)(2,1)} %param.24) | copy-start | bytes 2359300
  121.2 46.2 %all-gather.7.cloned.1.call-start = ((), (), s32[]{:S(2)}) async-start(), calls=%async_computation.12 | async-start | bytes 2359296 | tf_op jit(solution)/shard_map/all_gather | solution.py:518
  134.0 18.8 %copy-start.17 = (f32[512,768]{1,0:T(8,128)}, f32[512,768]{1,0:T(8,128)S(1)}, u32[]{:S(2)}) copy-start(f32[512,768]{1,0:T(8,128)S(1)} %get-tuple-element.1199) | copy-start | bytes 4718596
  134.1 18.7 %copy-start.42 = (f32[512]{0:T(512)}, f32[512]{0:T(512)S(1)}, u32[]{:S(2)}) copy-start(f32[512]{0:T(512)S(1)} %broadcast_multiply_fusion.6) | copy-start | bytes 6148
  134.8 18.0 %copy-start.48 = (f32[512]{0:T(512)}, f32[512]{0:T(512)S(1)}, u32[]{:S(2)}) copy-start(f32[512]{0:T(512)S(1)} %add_rsqrt_fusion) | copy-start | bytes 6148
  134.8 4.9 copy-start.25
  134.8 14.4 %slice-start = ((s8[4718592]{0:T(1024)(128)(4,1)}), s8[4194304]{0:T(1024)(128)(4,1)S(1)}, s32[]{:S(2)}) async-start(s8[4718592]{0:T(1024)(128)(4,1)} %bitcast.398), calls=%async_computation.18 | async-start | bytes 8388608
  139.7 9.5 %copy-start.59 = (f32[512,3072]{1,0:T(8,128)}, f32[512,3072]{1,0:T(8,128)S(1)}, u32[]{:S(2)}) copy-start(f32[512,3072]{1,0:T(8,128)S(1)} %fusion.125) | copy-start | bytes 18874372
  139.7 9.5 %slice-start.1 = ((s8[4718592]{0:T(1024)(128)(4,1)}), s8[524288]{0:T(1024)(128)(4,1)S(1)}, s32[]{:S(2)}) async-start(s8[4718592]{0:T(1024)(128)(4,1)} %bitcast.398), calls=%async_computation.19 | async-start | bytes 1048576
  149.2 3.6 copy-start.60
  152.8 1.7 copy-start.52
  156.3 135.3 %reduce-scatter.21.cloned.1.call-start = ((), (), s32[]{:S(2)}) async-start(), calls=%async_computation.9 | async-start | bytes 2359296 | tf_op jit(solution)/shard_map/reduce_scatter | solution.py:549
  176.8 2.9 copy-start.4
  179.7 1.9 copy-start.9
  187.2 2.9 copy-start.4
  190.1 1.9 copy-start.9
  204.8 2.5 copy-start.5
  207.3 6.4 %copy-start.10 = (bf16[2,512,12,64]{1,3,2,0:T(8,128)(2,1)S(1)}, bf16[2,512,12,64]{1,3,2,0:T(8,128)(2,1)}, u32[]{:S(2)}) copy-start(bf16[2,512,12,64]{1,3,2,0:T(8,128)(2,1)} %get-tuple-element.1769) | copy-start | bytes 4718596 | tf_op jit(solution)/shard_map/while
  207.3 6.4 %copy-start.21 = (f32[512,12,64]{0,2,1:T(8,128)S(1)}, f32[512,12,64]{0,2,1:T(8,128)}, u32[]{:S(2)}) copy-start(f32[512,12,64]{0,2,1:T(8,128)} %get-tuple-element.1739) | copy-start | bytes 4718596 | tf_op jit(solution)/shard_map/while
  209.2 4.5 copy-start.2
  217.3 9.2 %copy-start.22 = (f32[512,12,64]{0,2,1:T(8,128)}, f32[512,12,64]{0,2,1:T(8,128)S(1)}, u32[]{:S(2)}) copy-start(f32[512,12,64]{0,2,1:T(8,128)S(1)} %bitcast_add_fusion.5) | copy-start | bytes 4718596 | tf_op jit(solution)/shard_map/while
  240.3 2.5 copy-start.5
  242.8 6.4 %copy-start.10 = (bf16[2,512,12,64]{1,3,2,0:T(8,128)(2,1)S(1)}, bf16[2,512,12,64]{1,3,2,0:T(8,128)(2,1)}, u32[]{:S(2)}) copy-start(bf16[2,512,12,64]{1,3,2,0:T(8,128)(2,1)} %get-tuple-element.1769) | copy-start | bytes 4718596 | tf_op jit(solution)/shard_map/while
  242.8 6.4 %copy-start.21 = (f32[512,12,64]{0,2,1:T(8,128)S(1)}, f32[512,12,64]{0,2,1:T(8,128)}, u32[]{:S(2)}) copy-start(f32[512,12,64]{0,2,1:T(8,128)} %get-tuple-element.1739) | copy-start | bytes 4718596 | tf_op jit(solution)/shard_map/while
  244.7 4.5 copy-start.2
  252.9 9.2 %copy-start.22 = (f32[512,12,64]{0,2,1:T(8,128)}, f32[512,12,64]{0,2,1:T(8,128)S(1)}, u32[]{:S(2)}) copy-start(f32[512,12,64]{0,2,1:T(8,128)S(1)} %bitcast_add_fusion.5) | copy-start | bytes 4718596 | tf_op jit(solution)/shard_map/while
  275.0 58.0 %reduce-scatter.31.cloned.1.call-start = ((), (), s32[]{:S(2)}) async-start(), calls=%async_computation.16 | async-start | bytes 1769472
  279.4 2.6 copy-start.6
  281.9 53.5 %reduce-scatter.27.cloned.1.call-start = ((), (), s32[]{:S(2)}) async-start(), calls=%async_computation.14 | async-start | bytes 1769472
  285.4 2.6 copy-start.23
  287.9 48.8 %reduce-scatter.29.cloned.1.call-start = ((), (), s32[]{:S(2)}) async-start(), calls=%async_computation.15 | async-start | bytes 1769472
  291.6 61.6 %reduce-scatter.25.cloned.1.call-start = ((), (), s32[]{:S(2)}) async-start(), calls=%async_computation.13 | async-start | bytes 1769472
  295.3 60.2 %reduce-scatter.33.cloned.1.call-start = ((), (), s32[]{:S(2)}) async-start(), calls=%async_computation.17 | async-start | bytes 7077888
  310.7 1.4 copy-start.49
  310.7 55.3 %reduce-scatter.23.cloned.1.call-start = ((), (), s32[]{:S(2)}) async-start(), calls=%async_computation.10 | async-start | bytes 7077888 | tf_op jit(solution)/shard_map/reduce_scatter | solution.py:588
  322.1 8.9 %copy-start.27 = (bf16[512,12,64]{0,2,1:T(8,128)(2,1)S(1)}, bf16[512,12,64]{0,2,1:T(8,128)(2,1)}, u32[]{:S(2)}) copy-start(bf16[512,12,64]{0,2,1:T(8,128)(2,1)} %copy-done.26) | copy-start | bytes 2359300
  322.1 8.9 %copy-start.53 = (bf16[768,768]{1,0:T(8,128)(2,1)S(1)}, bf16[768,768]{1,0:T(8,128)(2,1)}, u32[]{:S(2)}) copy-start(bf16[768,768]{1,0:T(8,128)(2,1)} %param.30) | copy-start | bytes 3538948
  338.1 1.8 copy-start.54
  338.1 1.8 copy-start.55
  340.0 1.7 copy-start.24
  340.0 1.7 copy-start.46
  341.6 8.7 %copy-start.13 = (f32[512,768]{1,0:T(8,128)S(1)}, f32[512,768]{1,0:T(8,128)}, u32[]{:S(2)}) copy-start(f32[512,768]{1,0:T(8,128)} %copy-done.11) | copy-start | bytes 4718596
  473.0 7.6 %copy-start.29 = (f32[48,3072]{1,0:T(8,128)S(1)}, f32[48,3072]{1,0:T(8,128)}, u32[]{:S(2)}) copy-start(f32[48,3072]{1,0:T(8,128)} %get-tuple-element.1802) | copy-start | bytes 1769476
  473.0 8.4 %copy-start.28 = (f32[192,768]{1,0:T(8,128)S(1)}, f32[192,768]{1,0:T(8,128)}, u32[]{:S(2)}) copy-start(f32[192,768]{1,0:T(8,128)} %get-tuple-element.1803) | copy-start | bytes 1769476
  (24 other events, 24.5 us)
Sparse Core Ops, SparseCore 0:
  13.5 12.2 all-gather.4
  121.4 10.2 reduce-scatter.18
  156.4 10.9 all-gather.6
  275.1 10.2 reduce-scatter.20
  287.5 9.8 reduce-scatter.30
  299.6 9.8 reduce-scatter.26
  311.7 9.8 reduce-scatter.28
  323.9 9.8 reduce-scatter.24
  336.1 13.7 reduce-scatter.32
  352.1 13.7 reduce-scatter.22
